TPU v7x, 32 devices: a whole 2x2x4 slice. The times are simulated.
32 devices in a mesh: batch: 4 (over x, core), cache: 8 (over z, y).
Axes of the slice: x: 2, y: 2, z: 4, core: 2. Of those that a mesh axis runs over, the one named last changes fastest.
Arguments:
- arrivals: bfloat16 [16, 4, 4096], P('batch', None, 'cache'), may hold values from -6 to 6
- norm_gain: float32 [4096], replicated, may hold values from 0.25 to 1.75
- qkv_weight: bfloat16 [4096, 6144], P(None, 'cache'), may hold values from -0.09375 to 0.09375
- out_weight: bfloat16 [4096, 4096], P('cache'), may hold values from -0.09375 to 0.09375
- kv_cache: bfloat16 [16, 16, 2, 8, 128, 128], P('batch', 'cache'), as said below
- slot: int32 [16], replicated, may hold values from 0 to 15, each once
- positions: int32 [16], P('batch'), may hold values from 1664 to 2044
- tile_lists: int32 [16, 8], P('batch'), may hold values from 0 to 15, as said below
Outputs:
- attended: bfloat16 [16, 4, 4096], P('batch', None, 'cache')
Inputs may be any that keep to these rules, and one draw needn't show every extreme that they name: `tile_lists`: tiles of a row are distinct; the first is the tile of position positions - 1, the others lie at most 12 tiles before it. `kv_cache`: entries are of magnitude at most 240.
All inputs are finite; a program needn't handle non-finite values.
Results may differ from a plain program's by a relative error of at most 0.022.
Values may be sent and summed in bfloat16 or wider, within the bound.
A program may use at most 64 MiB of HBM per device.

v0:
```python
import math
import jax
import jax.numpy as jnp
from jax import lax
from jax.sharding import PartitionSpec as P

HEADS = 32
KVH = 8
HD = 128
TILE = 128
IMW = 64
CW = 16
epsilon = 1e-05
very_low = -1e30


def window_mask(query_pos, key_pos):
    return jnp.abs(key_pos % IMW - query_pos % IMW) <= CW


def shards(arrivals, norm_gain, qkv_weight, out_weight, kv_cache, slot, positions, tile_lists):
    row_count = positions.shape[0]
    step_count = arrivals.shape[1]
    groups = HEADS // KVH
    head_share = out_weight.shape[0] // HD
    head_start = lax.axis_index("cache") * head_share
    everyone = lax.all_gather(arrivals, "batch", axis=0, tiled=True)
    inverse = jnp.argsort(slot)
    my_rows = lax.dynamic_slice_in_dim(inverse, lax.axis_index("batch") * row_count, row_count)
    picked = jnp.take(everyone, my_rows, axis=0)
    whole = lax.all_gather(picked, "cache", axis=2, tiled=True)
    wide_values = whole.astype(jnp.float32)
    normed = (
        wide_values
        * lax.rsqrt(jnp.mean(wide_values * wide_values, axis=-1, keepdims=True) + epsilon)
        * norm_gain
    ).astype(jnp.bfloat16)
    projected = jnp.dot(
        normed.reshape(row_count * step_count, -1), qkv_weight, preferred_element_type=jnp.float32
    )
    projected = projected.astype(jnp.bfloat16).reshape(row_count, step_count, -1)
    heads_all = lax.all_gather(projected, "cache", axis=2, tiled=True).reshape(
        row_count, step_count, KVH, groups + 2, HD
    )
    queries = heads_all[:, :, :, :groups, :]
    new_keys = heads_all[:, :, :, groups, :]
    new_vals = heads_all[:, :, :, groups + 1, :]
    score_scale = 1.0 / math.sqrt(HD)
    tiles_here = kv_cache.shape[1]
    tile_ids = lax.axis_index("cache") * tiles_here + jnp.arange(tiles_here, dtype=jnp.int32)
    listed = jnp.any(tile_lists[:, :, None] == tile_ids[None, None, :], axis=1)
    key_pos = tile_ids[:, None] * TILE + jnp.arange(TILE, dtype=jnp.int32)[None, :]
    step_index = jnp.arange(step_count, dtype=jnp.int32)
    query_pos = positions[:, None] + step_index[None, :]
    key_valid = listed[:, None, :, None] & (key_pos[None, None] < positions[:, None, None, None])
    key_valid = key_valid & window_mask(query_pos[:, :, None, None], key_pos[None, None])
    valid_wide = key_valid[:, None, None]
    scores = (
        jnp.einsum(
            "bsjgd,btjkd->bjgstk", queries, kv_cache[:, :, 0], preferred_element_type=jnp.float32
        )
        * score_scale
    )
    new_valid = (step_index[None, :, None] >= step_index[None, None, :]) & window_mask(
        query_pos[:, :, None], query_pos[:, None, :]
    )
    new_scores = (
        jnp.einsum("bsjgd,bujd->bjgsu", queries, new_keys, preferred_element_type=jnp.float32)
        * score_scale
    )
    new_max = jnp.max(jnp.where(new_valid[:, None, None], new_scores, -jnp.inf), axis=-1)
    local_max = jnp.max(jnp.where(valid_wide, scores, very_low), axis=(-2, -1))
    values_here = kv_cache[:, :, 1]

    def own_heads(array):
        merged = array.reshape((row_count, HEADS) + array.shape[3:])
        return lax.dynamic_slice_in_dim(merged, head_start, head_share, 1)

    weights = jnp.where(valid_wide, jnp.exp(scores - local_max[..., None, None]), 0.0)
    totals = jnp.sum(weights, axis=(-2, -1))
    numerator = jnp.einsum(
        "bjgstk,btjkd->bjgsd",
        weights.astype(jnp.bfloat16),
        values_here,
        preferred_element_type=jnp.float32,
    )
    part_sums, part_totals, part_peaks = (
        lax.all_to_all(
            numerator.reshape(1, row_count, HEADS, step_count, HD).astype(jnp.bfloat16),
            "cache",
            split_axis=2,
            concat_axis=0,
            tiled=True,
        ).astype(jnp.float32),
        lax.all_to_all(
            totals.reshape(1, row_count, HEADS, step_count).astype(jnp.bfloat16),
            "cache",
            split_axis=2,
            concat_axis=0,
            tiled=True,
        ).astype(jnp.float32),
        lax.all_to_all(
            local_max.reshape(1, row_count, HEADS, step_count).astype(jnp.bfloat16),
            "cache",
            split_axis=2,
            concat_axis=0,
            tiled=True,
        ).astype(jnp.float32),
    )
    top_own = jnp.maximum(jnp.max(part_peaks, axis=0), own_heads(new_max))
    factor = jnp.exp(part_peaks - top_own[None])
    numer_own = jnp.sum(part_sums * factor[..., None], axis=0)
    total_own = jnp.sum(part_totals * factor, axis=0)
    own_new = own_heads(new_scores)
    new_weights = jnp.where(new_valid[:, None], jnp.exp(own_new - top_own[..., None]), 0.0)
    own_vals = lax.dynamic_slice_in_dim(
        jnp.repeat(new_vals, groups, axis=2), head_start, head_share, 2
    )
    total_all = total_own + jnp.sum(new_weights, axis=-1)
    numer_all = numer_own + jnp.einsum(
        "bhsu,buhd->bhsd",
        new_weights.astype(jnp.bfloat16),
        own_vals,
        preferred_element_type=jnp.float32,
    )
    attention = (numer_all / total_all[..., None]).astype(jnp.bfloat16)
    attn_flat = attention.transpose(0, 2, 1, 3).reshape(row_count * step_count, head_share * HD)
    partial_out = jnp.dot(attn_flat, out_weight, preferred_element_type=jnp.float32).reshape(
        row_count, step_count, -1
    )
    return lax.psum_scatter(
        partial_out.astype(jnp.bfloat16), "cache", scatter_dimension=2, tiled=True
    )


def solution(mesh):
    in_specs = (
        P("batch", None, "cache"),
        P(),
        P(None, "cache"),
        P("cache", None),
        P("batch", "cache", None, None, None, None),
        P(),
        P("batch"),
        P("batch", None),
    )
    out_specs = P("batch", None, "cache")
    return jax.shard_map(shards, mesh=mesh, in_specs=in_specs, out_specs=out_specs, check_vma=False)
```

profile of v0, /device:TPU:0, one launch (start us, length us, event | category | flops | bytes accessed | tf_op | source)
XLA Modules:
  0.0 208.3 jit_solution(18391242171131757612)
XLA Ops:
  6.5 0.9 compare_reduce_fusion
  7.4 0.1 copy.89
  7.5 0.7 add_select_fusion
  8.4 1.9 sort.17
  10.3 6.5 %all_gather.9 = bf16[16,4,512]{2,1,0:T(4,128)(2,1)S(1)} all-gather(bf16[4,4,512]{2,1,0:T(4,128)(2,1)} %param.8), channel_id=1, replica_groups=mesh['batch'=4,'cache'=8] {'batch'}, dimensions={0}, use_global_device_ids=true | all-gather | bytes 81920 | tf_op jit(solution)/shard_map/all_gather | solution.py:27
  16.8 0.6 gather_fusion
  17.4 0.1 broadcast_select_fusion
  17.5 31.3 %all_gather.10 = bf16[4,4,4096]{2,1,0:T(4,128)(2,1)S(1)} all-gather(bf16[4,4,512]{2,1,0:T(4,128)(2,1)S(1)} %broadcast_select_fusion), channel_id=1, replica_groups=mesh['batch'=4,'cache'=8] {'cache'}, dimensions={2}, use_global_device_ids=true | all-gather | bytes 147456 | tf_op jit(solution)/shard_map/all_gather | solution.py:31
  48.8 0.2 fusion.14
  49.0 0.9 fusion.16
  49.9 3.7 %convolution_convert_fusion.1 = bf16[16,768]{1,0:T(8,128)(2,1)S(1)} fusion(bf16[16,4096]{1,0:T(8,128)(2,1)S(1)} %reshape.312, bf16[4096,768]{1,0:T(8,128)(2,1)} %param.10), kind=kOutput, calls=%fused_computation.13 | convolution fusion | flops 100675584 | bytes 6447104 | tf_op jit(solution)/shard_map/dot_general | solution.py:38
  53.6 30.7 %all_gather.11 = bf16[4,4,6144]{2,1,0:T(4,128)(2,1)S(1)} all-gather(bf16[4,4,768]{2,1,0:T(4,128)(2,1)S(1)} %reshape.313), channel_id=1, replica_groups=mesh['batch'=4,'cache'=8] {'cache'}, dimensions={2}, use_global_device_ids=true | all-gather | bytes 221184 | tf_op jit(solution)/shard_map/all_gather | solution.py:42
  84.3 0.2 reshape.314
  84.5 2.6 %fusion.37 = (bf16[4,2,1,8,128,128]{5,4,3,2,1,0:T(8,128)(2,1)S(1)}, bf16[4,2,1,8,128,128]{5,4,3,2,1,0:T(8,128)(2,1)S(1)}) fusion(bf16[4,2,2,8,128,128]{5,4,3,2,1,0:T(8,128)(2,1)} %param.12), kind=kLoop, calls=%fused_computation.74 | loop fusion | bytes 8388608 | tf_op jit(solution)/shard_map/slice | solution.py:73
  87.3 0.1 compare_and_fusion
  87.4 0.8 select_reduce_fusion
  88.1 0.2 copy.95
  88.3 0.8 copy.116
  89.1 5.5 %all-to-all-start.1 = ((bf16[1,4,32,4]{3,1,0,2:T(4,128)(2,1)}), bf16[1,4,32,4]{3,1,0,2:T(4,128)(2,1)S(1)}, u32[]{:S(2)}, u32[]{:S(2)}) async-start(bf16[1,4,32,4]{3,1,0,2:T(4,128)(2,1)} %bitcast.15), calls=%async_computation.1 | async-start | bytes 65536 | tf_op jit(solution)/shard_map/all_to_all | solution.py:102
  94.6 0.1 fusion.38
  94.8 0.5 fusion.12
  95.3 0.4 fusion.7
  95.7 1.3 select_reduce_fusion.1
  97.1 0.1 reshape.315
  97.2 0.1 copy.102
  97.3 0.1 reshape.316
  97.4 0.2 copy.106
  97.6 0.7 copy.94
  98.3 0.8 copy.120
  99.1 2.2 %all-to-all-done.1 = bf16[1,4,32,4]{3,1,0,2:T(4,128)(2,1)S(1)} async-done(((bf16[1,4,32,4]{3,1,0,2:T(4,128)(2,1)}), bf16[1,4,32,4]{3,1,0,2:T(4,128)(2,1)S(1)}, u32[]{:S(2)}, u32[]{:S(2)}) %all-to-all-start.1) | async-done | bytes 1056 | tf_op jit(solution)/shard_map/all_to_all | solution.py:102
  101.3 3.8 %all-to-all-start.2 = ((bf16[1,4,32,4]{3,1,0,2:T(4,128)(2,1)}), bf16[1,4,32,4]{3,1,0,2:T(4,128)(2,1)S(1)}, u32[]{:S(2)}, u32[]{:S(2)}) async-start(bf16[1,4,32,4]{3,1,0,2:T(4,128)(2,1)} %bitcast.26), calls=%async_computation.2 | async-start | bytes 65536 | tf_op jit(solution)/shard_map/all_to_all | solution.py:95
  105.1 0.3 copy.117
  105.4 6.3 %all-to-all-done.2 = bf16[1,4,32,4]{3,1,0,2:T(4,128)(2,1)S(1)} async-done(((bf16[1,4,32,4]{3,1,0,2:T(4,128)(2,1)}), bf16[1,4,32,4]{3,1,0,2:T(4,128)(2,1)S(1)}, u32[]{:S(2)}, u32[]{:S(2)}) %all-to-all-start.2) | async-done | bytes 1056 | tf_op jit(solution)/shard_map/all_to_all | solution.py:95
  111.8 3.4 %all-to-all-start = ((bf16[1,4,32,4,128]{4,3,1,0,2:T(4,128)(2,1)}), bf16[1,4,32,4,128]{4,3,1,0,2:T(4,128)(2,1)S(1)}, u32[]{:S(2)}, u32[]{:S(2)}) async-start(bf16[1,4,32,4,128]{4,3,1,0,2:T(4,128)(2,1)} %copy.94), calls=%async_computation | async-start | bytes 262144 | tf_op jit(solution)/shard_map/all_to_all | solution.py:88
  115.2 0.1 copy.109
  115.4 0.1 dynamic-slice_maximum_fusion
  115.5 0.1 fusion.27
  115.6 0.2 copy.104
  115.9 0.1 copy.110
  116.0 0.3 copy.101
  116.3 6.1 %all-to-all-done = bf16[1,4,32,4,128]{4,3,1,0,2:T(4,128)(2,1)S(1)} async-done(((bf16[1,4,32,4,128]{4,3,1,0,2:T(4,128)(2,1)}), bf16[1,4,32,4,128]{4,3,1,0,2:T(4,128)(2,1)S(1)}, u32[]{:S(2)}, u32[]{:S(2)}) %all-to-all-start) | async-done | bytes 131104 | tf_op jit(solution)/shard_map/all_to_all | solution.py:88
  122.4 0.2 fusion.17
  122.7 3.0 %convolution_convert_fusion = bf16[4,4,4096]{2,1,0:T(4,128)(2,1)S(1)} fusion(bf16[512,4096]{1,0:T(8,128)(2,1)} %param.11, bf16[4,4,4,4]{3,2,1,0:T(4,128)(2,1)S(1)} %copy.104, f32[4,4,4,128]{3,2,0,1:T(4,128)S(1)} %fusion.17, f32[4,4,4]{1,2,0:T(4,128)S(1)} %copy.110, bf16[4,4,32,128]{3,1,2,0:T(4,128)(2,1)S(1)} %bitcast.113, s32[]{:T(128)S(6)} %select_n.81), kind=kOutput, calls=%fused_computation.1 | convolution fusion | flops 67264512 | bytes 4399108 | tf_op jit(solution)/shard_map/dot_general | solution.py:128
  125.7 4.8 %copy.121 = bf16[4,4,4096]{1,0,2:T(4,128)(2,1)} copy(bf16[4,4,4096]{2,1,0:T(4,128)(2,1)S(1)} %convolution_convert_fusion) | data formatting | bytes 262144
  130.5 6.1 %reshape.338 = bf16[4096,16]{1,0:T(8,128)(2,1)} reshape(bf16[4096,4,4]{2,1,0:T(4,128)(2,1)} %bitcast.110) | data formatting | bytes 262144
  136.6 62.8 %reduce-scatter.4.cloned.1.call-done = bf16[512,16]{1,0:T(8,128)(2,1)} async-done(((bf16[4096,16]{1,0:T(8,128)(2,1)}), bf16[512,16]{1,0:T(8,128)(2,1)}) %reduce-scatter.4.cloned.1.call-update) | async-done | bytes 16400
  199.3 1.1 reshape.339
  200.5 0.9 copy.122
  (22 shorter events, 0.7 us)
Async XLA Ops:
  84.5 2.6 %copy-start = (s32[4]{0:T(128)S(1)}, s32[4]{0:T(128)}, u32[]{:S(2)}) copy-start(s32[4]{0:T(128)} %param.14) | copy-start | bytes 52
  89.1 12.2 %all-to-all-start.1 = ((bf16[1,4,32,4]{3,1,0,2:T(4,128)(2,1)}), bf16[1,4,32,4]{3,1,0,2:T(4,128)(2,1)S(1)}, u32[]{:S(2)}, u32[]{:S(2)}) async-start(bf16[1,4,32,4]{3,1,0,2:T(4,128)(2,1)} %bitcast.15), calls=%async_computation.1 | async-start | bytes 65536 | tf_op jit(solution)/shard_map/all_to_all | solution.py:102
  101.3 10.5 %all-to-all-start.2 = ((bf16[1,4,32,4]{3,1,0,2:T(4,128)(2,1)}), bf16[1,4,32,4]{3,1,0,2:T(4,128)(2,1)S(1)}, u32[]{:S(2)}, u32[]{:S(2)}) async-start(bf16[1,4,32,4]{3,1,0,2:T(4,128)(2,1)} %bitcast.26), calls=%async_computation.2 | async-start | bytes 65536 | tf_op jit(solution)/shard_map/all_to_all | solution.py:95
  111.8 10.7 %all-to-all-start = ((bf16[1,4,32,4,128]{4,3,1,0,2:T(4,128)(2,1)}), bf16[1,4,32,4,128]{4,3,1,0,2:T(4,128)(2,1)S(1)}, u32[]{:S(2)}, u32[]{:S(2)}) async-start(bf16[1,4,32,4,128]{4,3,1,0,2:T(4,128)(2,1)} %copy.94), calls=%async_computation | async-start | bytes 262144 | tf_op jit(solution)/shard_map/all_to_all | solution.py:88
  115.1 84.2 %reduce-scatter.4.cloned.1.call-start = ((), (), s32[]{:S(2)}) async-start(), calls=%async_computation.4 | async-start | bytes 1179648
Sparse Core Ops, SparseCore 0:
  136.7 62.6 reduce-scatter.3
where the time goes:
time: 209 us; the launch traced here: 208 us
  waiting for transfers between devices  77.5 us (37%)
  blocking collectives  68.5 us (33%)
  local copies, waits for them, and re-layouts  20.8 us (10%)
  between operations  13.6 us (7%)
  starting transfers between devices  12.7 us (6%)
  matrix products  9.2 us (4%)
  other arithmetic  6.06 us (3%)
    unnamed x2, waiting for transfers between devices  62.8 us
    all_gather x1, blocking collectives, shards(): whole = lax.all_gather(picked, 'cache', axis=2, tiled=True)  31.3 us
    all_gather x1, blocking collectives, shards(): lax.all_gather(projected, 'cache', axis=2, tiled=True)  30.7 us
    unnamed x6, local copies, waits for them, and re-layouts  12.9 us
    all_gather x1, blocking collectives, shards(): everyone = lax.all_gather(arrivals, 'batch', axis=0, tiled=True)  6.46 us
    all_to_all x1, waiting for transfers between devices, shards(): lax.all_to_all(totals.reshape(1, row_count, HEADS, step_count).astype(jnp...  6.33 us
    all_to_all x1, waiting for transfers between devices, shards(): lax.all_to_all(numerator.reshape(1, row_count, HEADS, step_count, HD).ast...  6.14 us
    all_to_all x1, starting transfers between devices, shards(): lax.all_to_all(local_max.reshape(1, row_count, HEADS, step_count).astype(...  5.49 us
  transfers between devices with their start and end apart: 4, of which 4 were waited for; matrix products, arithmetic and copies ran while one was open for 3% of the time, Pallas kernels for 0%

commit v1 on v0

--- a/solution.py
+++ b/solution.py
@@ -14,6 +14,24 @@
 very_low = -1e30
 
 
+def joined_along(pieces, dim):
+    dims = list(pieces.shape[1:])
+    dims[dim] *= pieces.shape[0]
+    return jnp.moveaxis(pieces, 0, dim).reshape(dims)
+
+
+def grow_blocks(array, axis):
+    size = lax.axis_size(axis)
+    blocks = array[None]
+    for level in range(size.bit_length() - 1):
+        distance = 1 << level
+        received = lax.ppermute(blocks, axis, [(i, i ^ distance) for i in range(size)])
+        both = jnp.stack([blocks, received])
+        upper = lax.axis_index(axis) >> level & 1
+        blocks = jnp.where(upper == 0, both, both[::-1]).reshape(-1, *array.shape)
+    return blocks
+
+
 def window_mask(query_pos, key_pos):
     return jnp.abs(key_pos % IMW - query_pos % IMW) <= CW
 
@@ -28,7 +46,7 @@
     inverse = jnp.argsort(slot)
     my_rows = lax.dynamic_slice_in_dim(inverse, lax.axis_index("batch") * row_count, row_count)
     picked = jnp.take(everyone, my_rows, axis=0)
-    whole = lax.all_gather(picked, "cache", axis=2, tiled=True)
+    whole = joined_along(grow_blocks(picked, "cache"), 2)
     wide_values = whole.astype(jnp.float32)
     normed = (
         wide_values

time: 209 us -> 192 us (0.919)
  blocking collectives: 68.5 us -> 38.1 us
  waiting for transfers between devices: 77.5 us -> 82.9 us
  starting transfers between devices: 12.7 us -> 17.6 us
    all_gather x1 -> x0, blocking collectives: 31.3 us -> none  [shards(): whole = lax.all_gather(picked, 'cache', axis=2, tiled=True)]
    ppermute x0 -> x3, starting transfers between devices: none -> 6.35 us  [grow_blocks(): lax.ppermute(blocks, axis, [(i, i ^ distance) for i in range(size)])]
    ppermute x0 -> x3, waiting for transfers between devices: none -> 4.82 us  [grow_blocks(): lax.ppermute(blocks, axis, [(i, i ^ distance) for i in range(size)])]
    unnamed x6 -> x9, local copies, waits for them, and re-layouts: 12.9 us -> 13.1 us
  transfers between devices with their start and end apart: 4 -> 7, of which waited for: 4 -> 6; matrix products, arithmetic and copies ran while one was open for 3% -> 6% of each run, Pallas kernels for 0% -> 0%
where the time goes in v1:
time: 192 us; the launch traced here: 191 us
  waiting for transfers between devices  82.9 us (43%)
  blocking collectives  38.1 us (20%)
  local copies, waits for them, and re-layouts  22.6 us (12%)
  starting transfers between devices  17.6 us (9%)
  between operations  13.6 us (7%)
  matrix products  10.8 us (6%)
  other arithmetic  5.58 us (3%)
    unnamed x2, waiting for transfers between devices  62.8 us
    all_gather x1, blocking collectives, shards(): lax.all_gather(projected, 'cache', axis=2, tiled=True)  31.6 us
    unnamed x9, local copies, waits for them, and re-layouts  13.1 us
    all_gather x1, blocking collectives, shards(): everyone = lax.all_gather(arrivals, 'batch', axis=0, tiled=True)  6.46 us
    ppermute x3, starting transfers between devices, grow_blocks(): lax.ppermute(blocks, axis, [(i, i ^ distance) for i in range(size)])  6.35 us
    all_to_all x1, waiting for transfers between devices, shards(): lax.all_to_all(totals.reshape(1, row_count, HEADS, step_count).astype(jnp...  6.27 us
    all_to_all x1, waiting for transfers between devices, shards(): lax.all_to_all(numerator.reshape(1, row_count, HEADS, step_count, HD).ast...  6.14 us
    ppermute x3, waiting for transfers between devices, grow_blocks(): lax.ppermute(blocks, axis, [(i, i ^ distance) for i in range(size)])  4.82 us
  transfers between devices with their start and end apart: 7, of which 6 were waited for; matrix products, arithmetic and copies ran while one was open for 6% of the time, Pallas kernels for 0%

profile of v1, /device:TPU:0, one launch (start us, length us, event | category | flops | bytes accessed | tf_op | source)
XLA Modules:
  0.0 191.2 jit_solution(15933415007042894785)
XLA Ops:
  6.5 1.9 sort.17
  8.5 6.5 %all_gather.6 = bf16[16,4,512]{2,1,0:T(4,128)(2,1)S(1)} all-gather(bf16[4,4,512]{2,1,0:T(4,128)(2,1)} %param.8), channel_id=1, replica_groups=mesh['batch'=4,'cache'=8] {'batch'}, dimensions={0}, use_global_device_ids=true | all-gather | bytes 81920 | tf_op jit(solution)/shard_map/all_gather | solution.py:45
  15.0 0.6 gather_fusion
  15.6 2.1 %collective-permute-start = (bf16[1,4,4,512]{3,2,1,0:T(4,128)(2,1)S(1)}, bf16[1,4,4,512]{3,2,1,0:T(4,128)(2,1)S(1)}, u32[]{:S(2)}, u32[]{:S(2)}) collective-permute-start(bf16[1,4,4,512]{3,2,1,0:T(4,128)(2,1)S(1)} %bitcast_select_fusion), channel_id=1, source_target_pairs={{0,1},{1,0},{2,3},{3,2},{4,5},{5,4},{6,7},{7,6},{8,9},{9,8},{10,11... | collective-permute-start | bytes 49160 | tf_op jit(solution)/shard_map/ppermute | solution.py:28
  17.8 0.9 compare_reduce_fusion
  18.7 0.1 copy.94
  18.8 0.7 add_select_fusion
  19.6 4.0 %fusion.39 = (bf16[4,2,1,8,128,128]{5,4,3,2,1,0:T(8,128)(2,1)S(1)}, bf16[4,2,1,8,128,128]{5,4,3,2,1,0:T(8,128)(2,1)}) fusion(bf16[4,2,2,8,128,128]{5,4,3,2,1,0:T(8,128)(2,1)} %param.12), kind=kLoop, calls=%fused_computation.83 | loop fusion | bytes 8388608 | tf_op jit(solution)/shard_map/slice | solution.py:91
  23.9 1.6 collective-permute-start.1
  25.6 2.3 %collective-permute-done.1 = bf16[2,4,4,512]{3,2,1,0:T(4,128)(2,1)S(1)} collective-permute-done((bf16[2,4,4,512]{3,2,1,0:T(4,128)(2,1)S(1)}, bf16[2,4,4,512]{3,2,1,0:T(4,128)(2,1)S(1)}, u32[]{:S(2)}, u32[]{:S(2)}) %collective-permute-start.1) | collective-permute-done | bytes 32800 | tf_op jit(solution)/shard_map/ppermute | solution.py:28
  28.0 2.7 %collective-permute-start.2 = (bf16[4,4,4,512]{3,2,1,0:T(4,128)(2,1)S(1)}, bf16[4,4,4,512]{3,2,1,0:T(4,128)(2,1)S(1)}, u32[]{:S(2)}, u32[]{:S(2)}) collective-permute-start(bf16[4,4,4,512]{3,2,1,0:T(4,128)(2,1)S(1)} %bitcast.133), channel_id=1, source_target_pairs={{0,4},{1,5},{2,6},{3,7},{4,0},{5,1},{6,2},{7,3},{8,12},{9,13},{10,... | collective-permute-start | bytes 196616 | tf_op jit(solution)/shard_map/ppermute | solution.py:28
  30.7 2.5 %collective-permute-done.2 = bf16[4,4,4,512]{3,2,1,0:T(4,128)(2,1)S(1)} collective-permute-done((bf16[4,4,4,512]{3,2,1,0:T(4,128)(2,1)S(1)}, bf16[4,4,4,512]{3,2,1,0:T(4,128)(2,1)S(1)}, u32[]{:S(2)}, u32[]{:S(2)}) %collective-permute-start.2) | collective-permute-done | bytes 65568 | tf_op jit(solution)/shard_map/ppermute | solution.py:28
  33.3 0.2 multiply_reduce_fusion
  33.7 0.2 copy.122
  33.8 0.2 copy.135
  34.0 3.7 %convolution_convert_fusion.1 = bf16[16,768]{1,0:T(8,128)(2,1)S(1)} fusion(bf16[4096,768]{1,0:T(8,128)(2,1)} %param.10, f32[16,4096]{1,0:T(8,128)S(1)} %bitcast.131, f32[4096]{0:T(1024)S(1)} %copy-done, f32[16]{0:T(128)S(1)} %rsqrt.12), kind=kOutput, calls=%fused_computation.13 | convolution fusion | flops 100872192 | bytes 6594624 | tf_op jit(solution)/shard_map/dot_general | solution.py:56
  37.8 31.6 %all_gather.7 = bf16[4,4,6144]{2,1,0:T(4,128)(2,1)S(1)} all-gather(bf16[4,4,768]{2,1,0:T(4,128)(2,1)S(1)} %reshape.349), channel_id=1, replica_groups=mesh['batch'=4,'cache'=8] {'cache'}, dimensions={2}, use_global_device_ids=true | all-gather | bytes 221184 | tf_op jit(solution)/shard_map/all_gather | solution.py:60
  69.4 0.2 reshape.350
  69.6 0.1 fusion.40
  69.7 2.4 %select_reduce_fusion = (f32[4,8,4,4]{2,3,1,0:T(4,128)S(1)}, f32[4,8,4,4,2,128]{5,2,4,3,1,0:T(4,128)S(1)}) fusion(pred[4,4,2,128]{3,2,1,0:T(4,128)(4,1)S(1)} %compare_and_fusion, bf16[4,2,1,8,128,128]{5,4,3,2,1,0:T(8,128)(2,1)} %get-tuple-element.10, bf16[4,4,8,6,128]{4,3,2,1,0:T(8,128)(2,1)S(1)} %reshape.350), kind=kOutput, calls=%fused_computation.20 | convolution fusion | flops 33947136 | bytes 2762752 | tf_op jit(solution)/shard_map/bsjgd,btjkd->bjgstk/dot_general | solution.py:77
  72.1 0.2 copy.101
  72.3 0.5 fusion.12
  72.7 0.8 copy.123
  73.5 4.5 %all-to-all-start.1 = ((bf16[1,4,32,4]{3,1,0,2:T(4,128)(2,1)}), bf16[1,4,32,4]{3,1,0,2:T(4,128)(2,1)S(1)}, u32[]{:S(2)}, u32[]{:S(2)}) async-start(bf16[1,4,32,4]{3,1,0,2:T(4,128)(2,1)} %bitcast.26), calls=%async_computation.1 | async-start | bytes 65536 | tf_op jit(solution)/shard_map/all_to_all | solution.py:120
  78.0 0.4 fusion.7
  78.5 1.3 select_reduce_fusion.1
  80.0 0.1 reshape.352
  80.1 0.2 copy.112
  80.3 0.7 copy.100
  81.0 0.8 copy.127
  81.8 2.9 %all-to-all-done.1 = bf16[1,4,32,4]{3,1,0,2:T(4,128)(2,1)S(1)} async-done(((bf16[1,4,32,4]{3,1,0,2:T(4,128)(2,1)}), bf16[1,4,32,4]{3,1,0,2:T(4,128)(2,1)S(1)}, u32[]{:S(2)}, u32[]{:S(2)}) %all-to-all-start.1) | async-done | bytes 1056 | tf_op jit(solution)/shard_map/all_to_all | solution.py:120
  84.7 3.3 %all-to-all-start.2 = ((bf16[1,4,32,4]{3,1,0,2:T(4,128)(2,1)}), bf16[1,4,32,4]{3,1,0,2:T(4,128)(2,1)S(1)}, u32[]{:S(2)}, u32[]{:S(2)}) async-start(bf16[1,4,32,4]{3,1,0,2:T(4,128)(2,1)} %bitcast.37), calls=%async_computation.2 | async-start | bytes 65536 | tf_op jit(solution)/shard_map/all_to_all | solution.py:113
  88.0 0.3 copy.124
  88.4 6.3 %all-to-all-done.2 = bf16[1,4,32,4]{3,1,0,2:T(4,128)(2,1)S(1)} async-done(((bf16[1,4,32,4]{3,1,0,2:T(4,128)(2,1)}), bf16[1,4,32,4]{3,1,0,2:T(4,128)(2,1)S(1)}, u32[]{:S(2)}, u32[]{:S(2)}) %all-to-all-start.2) | async-done | bytes 1056 | tf_op jit(solution)/shard_map/all_to_all | solution.py:113
  94.7 3.4 %all-to-all-start = ((bf16[1,4,32,4,128]{4,3,1,0,2:T(4,128)(2,1)}), bf16[1,4,32,4,128]{4,3,1,0,2:T(4,128)(2,1)S(1)}, u32[]{:S(2)}, u32[]{:S(2)}) async-start(bf16[1,4,32,4,128]{4,3,1,0,2:T(4,128)(2,1)} %copy.100), calls=%async_computation | async-start | bytes 262144 | tf_op jit(solution)/shard_map/all_to_all | solution.py:106
  98.1 0.1 copy.115
  98.4 0.1 fusion.27
  98.6 0.2 copy.110
  98.8 0.1 copy.116
  98.9 0.3 copy.107
  99.2 6.1 %all-to-all-done = bf16[1,4,32,4,128]{4,3,1,0,2:T(4,128)(2,1)S(1)} async-done(((bf16[1,4,32,4,128]{4,3,1,0,2:T(4,128)(2,1)}), bf16[1,4,32,4,128]{4,3,1,0,2:T(4,128)(2,1)S(1)}, u32[]{:S(2)}, u32[]{:S(2)}) %all-to-all-start) | async-done | bytes 131104 | tf_op jit(solution)/shard_map/all_to_all | solution.py:106
  105.3 0.2 fusion.14
  105.6 3.0 %convolution_convert_fusion = bf16[4,4,4096]{2,1,0:T(4,128)(2,1)S(1)} fusion(bf16[512,4096]{1,0:T(8,128)(2,1)} %param.11, bf16[4,4,4,4]{3,2,1,0:T(4,128)(2,1)S(1)} %copy.110, f32[4,4,4,128]{3,2,0,1:T(4,128)S(1)} %fusion.14, f32[4,4,4]{1,2,0:T(4,128)S(1)} %copy.116, bf16[4,4,32,128]{3,1,2,0:T(4,128)(2,1)S(1)} %bitcast.135, s32[]{:T(128)S(6)} %select_n.128), kind=kOutput, calls=%fused_computation.1 | convolution fusion | flops 67264512 | bytes 4399108 | tf_op jit(solution)/shard_map/dot_general | solution.py:146
  108.6 4.8 %copy.128 = bf16[4,4,4096]{1,0,2:T(4,128)(2,1)} copy(bf16[4,4,4096]{2,1,0:T(4,128)(2,1)S(1)} %convolution_convert_fusion) | data formatting | bytes 262144
  113.4 6.1 %reshape.376 = bf16[4096,16]{1,0:T(8,128)(2,1)} reshape(bf16[4096,4,4]{2,1,0:T(4,128)(2,1)} %bitcast.127) | data formatting | bytes 262144
  119.5 62.8 %reduce-scatter.4.cloned.1.call-done = bf16[512,16]{1,0:T(8,128)(2,1)} async-done(((bf16[4096,16]{1,0:T(8,128)(2,1)}), bf16[512,16]{1,0:T(8,128)(2,1)}) %reduce-scatter.4.cloned.1.call-update) | async-done | bytes 16400
  182.2 1.1 reshape.377
  183.4 0.9 copy.129
  (37 shorter events, 1.5 us)
Async XLA Ops:
  15.6 8.2 %collective-permute-start = (bf16[1,4,4,512]{3,2,1,0:T(4,128)(2,1)S(1)}, bf16[1,4,4,512]{3,2,1,0:T(4,128)(2,1)S(1)}, u32[]{:S(2)}, u32[]{:S(2)}) collective-permute-start(bf16[1,4,4,512]{3,2,1,0:T(4,128)(2,1)S(1)} %bitcast_select_fusion), channel_id=1, source_target_pairs={{0,1},{1,0},{2,3},{3,2},{4,5},{5,4},{6,7},{7,6},{8,9},{9,8},{10,11... | collective-permute-start | bytes 49160 | tf_op jit(solution)/shard_map/ppermute | solution.py:28
  19.6 4.0 %copy-start.1 = (s32[4]{0:T(128)S(1)}, s32[4]{0:T(128)}, u32[]{:S(2)}) copy-start(s32[4]{0:T(128)} %param.14) | copy-start | bytes 52
  23.7 10.3 %copy-start = (f32[4096]{0:T(1024)S(1)}, f32[4096]{0:T(1024)}, u32[]{:S(2)}) copy-start(f32[4096]{0:T(1024)} %param.9) | copy-start | bytes 49156
  23.9 4.0 %collective-permute-start.1 = (bf16[2,4,4,512]{3,2,1,0:T(4,128)(2,1)S(1)}, bf16[2,4,4,512]{3,2,1,0:T(4,128)(2,1)S(1)}, u32[]{:S(2)}, u32[]{:S(2)}) collective-permute-start(bf16[2,4,4,512]{3,2,1,0:T(4,128)(2,1)S(1)} %get-tuple-element.20), channel_id=1, source_target_pairs={{0,2},{1,3},{2,0},{3,1},{4,6},{5,7},{6,4},{7,5},{8,10},{9,11},{10,... | collective-permute-start | bytes 98312 | tf_op jit(solution)/shard_map/ppermute | solution.py:28
  28.0 5.2 %collective-permute-start.2 = (bf16[4,4,4,512]{3,2,1,0:T(4,128)(2,1)S(1)}, bf16[4,4,4,512]{3,2,1,0:T(4,128)(2,1)S(1)}, u32[]{:S(2)}, u32[]{:S(2)}) collective-permute-start(bf16[4,4,4,512]{3,2,1,0:T(4,128)(2,1)S(1)} %bitcast.133), channel_id=1, source_target_pairs={{0,4},{1,5},{2,6},{3,7},{4,0},{5,1},{6,2},{7,3},{8,12},{9,13},{10,... | collective-permute-start | bytes 196616 | tf_op jit(solution)/shard_map/ppermute | solution.py:28
  73.5 11.2 %all-to-all-start.1 = ((bf16[1,4,32,4]{3,1,0,2:T(4,128)(2,1)}), bf16[1,4,32,4]{3,1,0,2:T(4,128)(2,1)S(1)}, u32[]{:S(2)}, u32[]{:S(2)}) async-start(bf16[1,4,32,4]{3,1,0,2:T(4,128)(2,1)} %bitcast.26), calls=%async_computation.1 | async-start | bytes 65536 | tf_op jit(solution)/shard_map/all_to_all | solution.py:120
  84.7 10.0 %all-to-all-start.2 = ((bf16[1,4,32,4]{3,1,0,2:T(4,128)(2,1)}), bf16[1,4,32,4]{3,1,0,2:T(4,128)(2,1)S(1)}, u32[]{:S(2)}, u32[]{:S(2)}) async-start(bf16[1,4,32,4]{3,1,0,2:T(4,128)(2,1)} %bitcast.37), calls=%async_computation.2 | async-start | bytes 65536 | tf_op jit(solution)/shard_map/all_to_all | solution.py:113
  94.7 10.7 %all-to-all-start = ((bf16[1,4,32,4,128]{4,3,1,0,2:T(4,128)(2,1)}), bf16[1,4,32,4,128]{4,3,1,0,2:T(4,128)(2,1)S(1)}, u32[]{:S(2)}, u32[]{:S(2)}) async-start(bf16[1,4,32,4,128]{4,3,1,0,2:T(4,128)(2,1)} %copy.100), calls=%async_computation | async-start | bytes 262144 | tf_op jit(solution)/shard_map/all_to_all | solution.py:106
  98.1 84.2 %reduce-scatter.4.cloned.1.call-start = ((), (), s32[]{:S(2)}) async-start(), calls=%async_computation.4 | async-start | bytes 1179648
Sparse Core Ops, SparseCore 0:
  119.6 62.6 reduce-scatter.3
